TPU v7x, 256 devices: a whole 4x4x8 slice. The times are simulated.
256 devices in a mesh: src: 32 (over y, z), dst: 8 (over x, core).
Axes of the slice: x: 4, y: 4, z: 8, core: 2. Of those that a mesh axis runs over, the one named last changes fastest.
Arguments:
- transition: bfloat16 [16384, 16384], P('src', 'dst'), may hold values from 5.4931641e-06 to 0.05
- emission: bfloat16 [8192, 16384], P('src', 'dst'), may hold values from 0.099609375 to 5
- forward: bfloat16 [3, 256, 16384], P(None, None, 'src'), may hold values from 0.25 to 4
- beta_end: bfloat16 [256, 16384], P(None, 'dst'), may hold values from 0.5 to 2
- scales: float32 [3, 256], replicated, may hold values from 0.5 to 2
- tokens: int32 [3, 256], replicated, may hold values from 0 to 8191
Outputs:
- counts: float32 [16384, 16384], P('src', 'dst')
- beta_first: float32 [256, 16384], P('dst', 'src')
All inputs are finite; a program needn't handle non-finite values.
Results may differ from a plain program's by a relative error of at most 0.00076.
Values may be sent and summed in bfloat16 or wider, within the bound.
A program may use at most 64 MiB of HBM per device.

v0:
```python
import jax
import jax.numpy as jnp
from jax import lax
from jax.sharding import PartitionSpec as P

B = 256
STEPS = 3


def local_rows(words, emission, first_word):
    keys = words - first_word
    table = (keys[:, None] == jnp.arange(emission.shape[0], dtype=jnp.int32)[None, :]).astype(
        jnp.bfloat16
    )
    return jnp.dot(table, emission, preferred_element_type=jnp.bfloat16)


def emitted_window(words, emission, first_word):
    return (
        lax.psum(local_rows(words, emission, first_word), "src")
        .astype(jnp.float32)
        .astype(jnp.bfloat16)
    )


def per_device(transition, emission, forward, beta_end, scales, tokens):
    steps = forward.shape[0]
    batch = forward.shape[1]
    src_cols = transition.shape[0]
    dst_cols = transition.shape[1]
    n_dst = lax.axis_size("dst")
    share = batch // n_dst
    first_word = lax.axis_index("src") * emission.shape[0]
    emitted_all = emitted_window(tokens.reshape(-1), emission, first_word).reshape(
        steps, batch, dst_cols
    )
    message = beta_end
    pairs = jnp.zeros((src_cols, dst_cols), jnp.float32)
    beta_first = jnp.zeros((share, src_cols), jnp.float32)
    for step in range(steps - 1, -1, -1):
        emitted = emitted_all[step]
        weighted = (
            emitted.astype(jnp.float32) * message.astype(jnp.float32) / scales[step][:, None]
        ).astype(jnp.bfloat16)
        pairs = pairs + lax.dot_general(
            forward[step], weighted, (((0,), (0,)), ((), ())), preferred_element_type=jnp.float32
        )
        partial_rows = lax.dot_general(
            weighted, transition, (((1,), (1,)), ((), ())), preferred_element_type=jnp.float32
        )
        summed = lax.psum(partial_rows, "dst")
        if step == 0:
            beta_first = lax.dynamic_slice_in_dim(summed, lax.axis_index("dst") * share, share, 0)
        else:
            gathered = lax.all_gather(summed.astype(jnp.bfloat16), "src", axis=1, tiled=True)
            message = lax.dynamic_slice_in_dim(
                gathered, lax.axis_index("dst") * dst_cols, dst_cols, 1
            )
    counts = transition.astype(jnp.float32) * pairs * (32.0 / (STEPS * B))
    return (counts, beta_first)


def solution(mesh):
    in_specs = (P("src", "dst"), P("src", "dst"), P(None, None, "src"), P(None, "dst"), P(), P())
    out_specs = (P("src", "dst"), P("dst", "src"))
    return jax.shard_map(
        per_device, mesh=mesh, in_specs=in_specs, out_specs=out_specs, check_vma=False
    )
```

profile of v0, /device:TPU:1, one launch (start us, length us, event | category | flops | bytes accessed | tf_op | source)
XLA Modules:
  0.0 516.1 jit_solution(17679597140141207824)
XLA Ops:
  7.2 0.0 all-reduce.5.cloned.1.call-start
  7.2 0.8 broadcast_subtract_fusion
  8.0 0.4 copy-done
  8.4 2.7 fusion.1
  11.1 0.0 all-reduce.5.cloned.1.call-update
  11.1 0.0 all-gather.3.cloned.1.call-start
  11.2 0.6 copy-done.7
  11.8 158.4 %all-reduce.5.cloned.1.call-done = bf16[768,2048]{1,0:T(8,128)(2,1)} async-done(((bf16[768,2048]{1,0:T(8,128)(2,1)}), bf16[768,2048]{1,0:T(8,128)(2,1)}) %all-reduce.5.cloned.1.call-update) | async-done | bytes 3145744 | tf_op jit(solution)/shard_map/psum | solution.py:20
  170.2 2.0 divide_convert_fusion.2
  172.1 1.0 copy-done.1
  173.2 1.5 fusion.12
  174.7 31.4 %all-reduce.8 = bf16[256,512]{1,0:T(8,128)(2,1)} all-reduce(f32[256,512]{1,0:T(8,128)} %fusion.12), channel_id=1, replica_groups=mesh['src'=32,'dst'=8] {'dst'}, use_global_device_ids=true, to_apply=%region_1.0 | all-reduce | flops 131072 | bytes 786432 | tf_op jit(solution)/shard_map/psum | solution.py:51
  206.1 0.0 all-gather.3.cloned.1.call-update
  206.1 0.0 all-gather.5.cloned.1.call-start
  206.2 97.7 %all-gather.3.cloned.1.call-done = bf16[256,16384]{1,0:T(8,128)(2,1)} async-done(((bf16[256,512]{1,0:T(8,128)(2,1)}), bf16[256,16384]{1,0:T(8,128)(2,1)}) %all-gather.3.cloned.1.call-update) | async-done | bytes 8388624 | tf_op jit(solution)/shard_map/all_gather | solution.py:55
  303.8 2.0 divide_convert_fusion.1
  305.8 0.9 copy-done.2
  306.8 1.5 fusion.13
  308.3 30.4 %all-reduce.9 = bf16[256,512]{1,0:T(8,128)(2,1)} all-reduce(f32[256,512]{1,0:T(8,128)} %fusion.13), channel_id=1, replica_groups=mesh['src'=32,'dst'=8] {'dst'}, use_global_device_ids=true, to_apply=%region_2.0 | all-reduce | flops 131072 | bytes 786432 | tf_op jit(solution)/shard_map/psum | solution.py:51
  338.7 0.0 all-gather.5.cloned.1.call-update
  338.7 0.0 all-reduce.7.cloned.1.call-start
  338.8 2.9 copy.8
  341.6 4.1 fusion.6
  345.8 3.7 fusion.4
  349.4 87.9 %all-gather.5.cloned.1.call-done = bf16[256,16384]{1,0:T(8,128)(2,1)} async-done(((bf16[256,512]{1,0:T(8,128)(2,1)}), bf16[256,16384]{1,0:T(8,128)(2,1)}) %all-gather.5.cloned.1.call-update) | async-done | bytes 8388624 | tf_op jit(solution)/shard_map/all_gather | solution.py:55
  437.4 2.1 divide_convert_fusion
  439.5 1.0 copy-done.4
  440.4 1.5 fusion.14
  442.0 6.9 %fusion = f32[512,2048]{0,1:T(8,128)} fusion(f32[2048,512]{1,0:T(8,128)} %fusion.6, f32[2048,512]{1,0:T(8,128)} %fusion.4, bf16[512,2048]{0,1:T(8,128)(2,1)S(1)} %copy.8, bf16[256,2048]{1,0:T(8,128)(2,1)} %copy-done.4, bf16[3,256,512]{2,1,0:T(8,128)(2,1)} %param.8), kind=kOutput, calls=%fused_computation.1 | convolution fusion | flops 542113792 | bytes 15990784 | tf_op jit(solution)/shard_map/dot_general | solution.py:45
  448.9 5.3 %copy.9 = f32[512,2048]{1,0:T(8,128)} copy(f32[512,2048]{0,1:T(8,128)} %fusion) | data formatting | bytes 8388608
  454.2 53.9 %all-reduce.7.cloned.1.call-done = f32[256,512]{1,0:T(8,128)} async-done(((f32[256,512]{1,0:T(8,128)}), f32[256,512]{1,0:T(8,128)}) %all-reduce.7.cloned.1.call-update) | async-done | bytes 524304 | tf_op jit(solution)/shard_map/psum | solution.py:51
  508.1 1.5 constant_dynamic-slice_fusion
  (14 shorter events, 0.1 us)
Async XLA Ops:
  7.2 1.2 copy-start
  7.2 163.0 %all-reduce.5.cloned.1.call-start = ((), (), s32[]{:S(2)}) async-start(), calls=%async_computation | async-start | bytes 6291456 | tf_op jit(solution)/shard_map/psum | solution.py:20
  11.1 0.7 copy-start.7
  11.1 162.1 %copy-start.5 = (bf16[512,2048]{1,0:T(8,128)(2,1)S(1)}, bf16[512,2048]{1,0:T(8,128)(2,1)}, u32[]{:S(2)}) copy-start(bf16[512,2048]{1,0:T(8,128)(2,1)} %param.6) | copy-start | bytes 6291460
  11.1 292.7 %all-gather.3.cloned.1.call-start = ((), (), s32[]{:S(2)}) async-start(), calls=%async_computation.1 | async-start | bytes 8650752 | tf_op jit(solution)/shard_map/all_gather | solution.py:55
  172.1 1.1 copy-start.1
  206.1 231.2 %all-gather.5.cloned.1.call-start = ((), (), s32[]{:S(2)}) async-start(), calls=%async_computation.2 | async-start | bytes 8650752 | tf_op jit(solution)/shard_map/all_gather | solution.py:55
  305.8 1.0 copy-start.2
  338.7 169.4 %all-reduce.7.cloned.1.call-start = ((), (), s32[]{:S(2)}) async-start(), calls=%async_computation.3 | async-start | bytes 1048576 | tf_op jit(solution)/shard_map/psum | solution.py:51
  341.6 4.1 copy-start.3
  437.4 3.1 copy-start.6
  439.5 1.0 copy-start.4
Sparse Core Ops, SparseCore 0:
  12.1 158.0 all-reduce.4
  206.2 97.5 all-gather.2
  338.8 98.4 all-gather.4
  442.1 65.9 all-reduce.6
where the time goes:
time: 518 us; the launch traced here: 516 us
  waiting for transfers between devices  398 us (77%)
  blocking collectives  61.7 us (12%)
  matrix products  22 us (4%)
  between operations  13.9 us (3%)
  local copies, waits for them, and re-layouts  13.7 us (3%)
  other arithmetic  6.79 us (1%)
    all_gather x2, waiting for transfers between devices, per_device(): lax.all_gather(summed.astype(jnp.bfloat16), 'src', axis=1, tiled=True)  186 us
    psum x1, waiting for transfers between devices, emitted_window(): lax.psum(local_rows(words, emission, first_word), 'src').astype(jnp.float32)  158 us
    psum x2, blocking collectives, per_device(): summed = lax.psum(partial_rows, 'dst')  61.7 us
    psum x1, waiting for transfers between devices, per_device(): summed = lax.psum(partial_rows, 'dst')  53.9 us
    dot_general x3, matrix products, per_device(): lax.dot_general(forward[step], weighted, (((0,), (0,)), ((), ())), prefer...  14.7 us
    unnamed x18, local copies, waits for them, and re-layouts  12.2 us
  transfers between devices with their start and end apart: 4, of which 4 were waited for; matrix products, arithmetic and copies ran while one was open for 4% of the time, Pallas kernels for 0%

commit v1 on v0

v1 whole, which is shorter than its diff:
```python
import jax
import jax.numpy as jnp
from jax import lax
from jax.experimental import pallas as pl
from jax.experimental.pallas import tpu as pltpu
from jax.sharding import PartitionSpec as P

MESH = pl.DeviceIdType.MESH
NX, NY, NZ, NC = 4, 4, 8, 2
B = 256
STEPS = 3
BF = jnp.bfloat16
F32 = jnp.float32


def dev(x, y, z, c):
    return (y * NZ + z, x * NC + c)


def kernel(
    trans, emis, forw, beta, scales, tokens,
    counts, first,
    tv, ev, fv, bv, ft, sc, tc,
    x2, rz2, x10, rz10, em_s, em,
    w, own, pb, pr, qb, orx, fp, fr, fq, fx, cb,
    l_sem, out_sem,
    e_s, e_r, z2_s, z2_r, zw_s, zw_r, z10_s, z10_r, pm_s, pm_r,
    y_s, y_r, pp_s, pp_r, o_s, o_r, zz_s, zz_r, fp_s, fp_r, fx_s, fx_r,
):
    s = lax.axis_index("src")
    d = lax.axis_index("dst")
    y, z = s // NZ, s % NZ
    x, c = d // NC, d % NC
    sib = 1 - c
    words = emis.shape[0]
    cols = emis.shape[1]
    blk = cols // 4
    rows = trans.shape[0]
    yo = pl.multiple_of(y * blk, blk)
    oc = z // 4
    q = z % 4
    qo = pl.multiple_of(q * blk, blk)
    is_owner = c == oc

    def zp(i):
        return lax.rem(z + i, NZ)

    def yp(i):
        return lax.rem(y + i, NY)

    def xp(i):
        return lax.rem(x + i, NX)

    barrier = pltpu.get_barrier_semaphore()
    peers = (
        [dev(x, y, z, sib)]
        + [dev(x, yp(i), z, c) for i in range(1, NY)]
        + [dev(x, y, zp(i), c) for i in range(1, NZ)]
        + [dev(xp(i), y, z, c) for i in range(1, NX)]
    )
    for p in peers:
        pl.semaphore_signal(barrier, inc=1, device_id=p, device_id_type=MESH)

    loads = [
        pltpu.make_async_copy(emis.at[:, pl.ds(yo, blk)], ev.at[y], l_sem.at[0]),
        pltpu.make_async_copy(
            beta.at[pl.ds(pl.multiple_of(z * 32, 32), 32), pl.ds(yo, blk)], bv, l_sem.at[1]
        ),
        pltpu.make_async_copy(trans, tv, l_sem.at[2]),
        pltpu.make_async_copy(forw, fv, l_sem.at[3]),
    ]
    for cp in loads:
        cp.start()

    pl.semaphore_wait(barrier, len(peers))

    sends = []

    def remote(src, dst, ss, rs, to):
        return pltpu.make_async_remote_copy(
            src_ref=src, dst_ref=dst, send_sem=ss, recv_sem=rs, device_id=to, device_id_type=MESH
        )

    def send(cp, cond=None):
        if cond is None:
            cp.start()
        else:
            pl.when(cond)(cp.start)
        sends.append((cond, cp))

    def arrive(cp, cond=None):
        if cond is None:
            cp.wait_recv()
        else:
            pl.when(cond)(cp.wait_recv)

    here = dev(x, y, z, sib)

    def landing(dst, rs):
        return remote(dst, dst, rs, rs, here)

    for i in (2, 1, 3):
        yt = yp(i)
        send(
            remote(
                emis.at[:, pl.ds(pl.multiple_of(yt * blk, blk), blk)],
                ev.at[y], e_s.at[i - 1], e_r.at[i - 1], dev(x, yt, z, c),
            )
        )

    eye = lax.broadcasted_iota(jnp.int32, (B, B), 0) == lax.broadcasted_iota(jnp.int32, (B, B), 1)
    for k in range(STEPS):
        for src, dst in ((scales[k : k + 1, :], sc), (tokens[k : k + 1, :].astype(F32), tc)):
            col = jnp.sum(jnp.where(eye, jnp.broadcast_to(src, (B, B)), 0.0), axis=1, keepdims=True)
            dst[k] = jnp.broadcast_to(col, (B, 128)).reshape(8, 32, 128)

    loads[3].wait()
    for k in range(STEPS):
        ft[:, k * B : (k + 1) * B] = fv[k].astype(F32).T.astype(BF)
    loads[2].wait()
    loads[1].wait()

    def lookup(k):
        tok = tc[k].reshape(B, 128)
        acc = jnp.zeros((B, blk), F32)
        for j in range(NY):
            base = ((j * NZ + z) * words).astype(F32)
            parts = []
            for t in range(words // 128):
                lane = lax.broadcasted_iota(jnp.int32, (B, 128), 1).astype(F32) + (base + 128.0 * t)
                parts.append(jnp.where(tok == lane, 1.0, 0.0).astype(BF))
            hot = jnp.concatenate(parts, axis=1)
            acc = acc + jnp.dot(hot, ev[j], preferred_element_type=F32)
        return acc.astype(BF).reshape(8, 32, blk)

    loads[0].wait()
    for i in (1, 3, 2):
        arrive(landing(ev.at[yp(NY - i)], e_r.at[i - 1]))
    x2[...] = lookup(2)
    for i in (4, 3, 5, 2, 6, 1, 7):
        send(remote(x2.at[zp(i)], rz2.at[i - 1], z2_s.at[i - 1], z2_r.at[i - 1], dev(x, y, zp(i), c)))
    for kk in range(2):
        x10[:, kk] = lookup(kk)

    tot = x2[z].astype(F32)
    for i in (1, 7, 2, 6, 3, 5, 4):
        arrive(landing(rz2.at[i - 1], z2_r.at[i - 1]))
        tot = tot + rz2[i - 1].astype(F32)

    def scaled(value, k, g):
        den = sc[k, g]
        return value / jnp.concatenate([den] * (blk // 128), axis=1)

    w[2, z // 2, z % 2, :, pl.ds(yo, blk)] = scaled(tot * bv[...].astype(F32), 2, z).astype(BF)
    mine = w.at[2, z // 2, z % 2, :, pl.ds(yo, blk)]
    for i in (4, 3, 5, 2, 6, 1, 7):
        send(remote(mine, mine, zw_s.at[i - 1], zw_r.at[i - 1], dev(x, y, zp(i), c)))
    for i in (1, 7, 2, 6, 3, 5, 4):
        zt = zp(NZ - i)
        arrive(landing(w.at[2, zt // 2, zt % 2, :, pl.ds(yo, blk)], zw_r.at[i - 1]))
    for h in range(2):
        part = w.at[2, :, h, :, pl.ds(yo, blk)]
        for i in (2, 1, 3):
            send(remote(part, part, y_s.at[2, h, i - 1], y_r.at[2, h, i - 1], dev(x, yp(i), z, c)))

    for i in (4, 3, 5, 2, 6, 1, 7):
        send(
            remote(x10.at[zp(i)], rz10.at[i - 1], z10_s.at[i - 1], z10_r.at[i - 1], dev(x, y, zp(i), c))
        )

    def wait_rows(k, h):
        for i in (1, 3, 2):
            yt = yp(NY - i)
            if k == 2:
                dst = w.at[2, :, h, :, pl.ds(pl.multiple_of(yt * blk, blk), blk)]
            else:
                dst = w.at[k, yt, h]
            arrive(landing(dst, y_r.at[k, h, i - 1]))

    def product(k, h, n):
        return lax.dot_general(
            w[k, :, h].reshape(B // 2, cols), tv[n * 256 : (n + 1) * 256, :],
            (((1,), (1,)), ((), ())), preferred_element_type=F32,
        )

    for k in (1, 0):
        for h in range(2):
            wait_rows(k + 1, h)
            for n in range(rows // 256):
                res = product(k + 1, h, n).reshape(4, 2, 16, 256)
                for cc in range(2):
                    own[k, h, cc, :, :, n * 256 : (n + 1) * 256] = res[:, cc]
                    pb[k, h, cc, :, :, n * 256 : (n + 1) * 256] = res[:, cc].astype(BF)
            send(
                remote(pb.at[k, h, sib], pr.at[k, h], pp_s.at[k, h], pp_r.at[k, h], dev(x, y, z, sib))
            )
        for h in range(2):
            arrive(landing(pr.at[k, h], pp_r.at[k, h]))
            qb[k, h] = (own[k, h, c] + pr[k, h].astype(F32)).astype(BF)
            for r in range(NY):
                self_r = (x == y) & (y == r) & is_owner
                send(
                    remote(
                        qb.at[k, h, r], orx.at[k, h, x, c], o_s.at[k, h, r], o_r.at[k, h, x * 2 + c],
                        dev(y, r, z, oc),
                    ),
                    jnp.logical_not(self_r),
                )

                @pl.when(self_r)
                def _():
                    orx[k, h, x, c] = qb[k, h, r]

        if k == 1:
            for kk in range(2):
                acc = x10[z, kk].astype(F32)
                for i in (1, 7, 2, 6, 3, 5, 4):
                    if kk == 0:
                        arrive(landing(rz10.at[i - 1], z10_r.at[i - 1]))
                    acc = acc + rz10[i - 1, kk].astype(F32)
                em_s[kk] = acc.astype(BF)
            pm_self = (y == z // 2) & (z == 4 * c + y)
            send(
                remote(em_s, em.at[z % 2], pm_s.at[0], pm_r.at[z % 2], dev(x, z // 2, 4 * c + y, c)),
                jnp.logical_not(pm_self),
            )

            @pl.when(pm_self)
            def _():
                em[z % 2] = em_s[...]

            for h in range(2):
                from_self = (y == q) & (z == 2 * y + h)
                arrive(landing(em.at[h], pm_r.at[h]), is_owner & jnp.logical_not(from_self))

        for h in range(2):
            for j in range(8):
                from_self = (x == y) & (x * 2 + c == j)
                arrive(
                    landing(orx.at[k, h, j // 2, j % 2], o_r.at[k, h, j]),
                    is_owner & jnp.logical_not(from_self),
                )

            @pl.when(is_owner)
            def _():
                halves = []
                for cc in range(2):
                    acc = orx[k, h, 0, cc].astype(F32)
                    for xx in range(1, NX):
                        acc = acc + orx[k, h, xx, cc].astype(F32)
                    halves.append(acc)
                msg = jnp.concatenate(halves, axis=0).astype(BF).astype(F32)
                w[k, y, h, :, pl.ds(qo, blk)] = scaled(
                    em[h, k].astype(F32) * msg, k, 2 * y + h
                ).astype(BF)

            tile = w.at[k, y, h, :, pl.ds(qo, blk)]
            for i in (4, 3, 5, 2, 6, 1, 7):
                send(
                    remote(tile, tile, zz_s.at[k, h, i - 1], zz_r.at[k, h, q], dev(x, y, zp(i), c)),
                    is_owner,
                )
        for h in range(2):
            for j in range(4):
                arrive(
                    landing(w.at[k, y, h, :, j * blk : (j + 1) * blk], zz_r.at[k, h, j]),
                    z != 4 * c + j,
                )
            part = w.at[k, y, h]
            for i in (2, 1, 3):
                send(remote(part, part, y_s.at[k, h, i - 1], y_r.at[k, h, i - 1], dev(x, yp(i), z, c)))

    for h in range(2):
        wait_rows(0, h)
        for n in range(rows // 256):
            fp[h, :, :, n * 256 : (n + 1) * 256] = product(0, h, n).reshape(4, 32, 256)
    send(remote(fp.at[sib], fr, fp_s.at[0], fp_r.at[0], dev(x, y, z, sib)))

    def count_block(n):
        lo = n * 256
        acc = jnp.dot(
            ft[...], w[:, :, :, :, lo : lo + 256].reshape(STEPS * B, 256), preferred_element_type=F32
        )
        cb[:, lo : lo + 256] = tv[:, lo : lo + 256].astype(F32) * acc * (32.0 / (STEPS * B))
        cp = pltpu.make_async_copy(
            cb.at[:, lo : lo + 256], counts.at[:, lo : lo + 256], out_sem.at[n]
        )
        cp.start()
        return cp

    outs = [count_block(n) for n in range(2)]
    arrive(landing(fr, fp_r.at[0]))
    fq[...] = fp[c] + fr[...]
    for i in (2, 1, 3):
        send(remote(fq.at[xp(i)], fx.at[i - 1], fx_s.at[i - 1], fx_r.at[i - 1], dev(xp(i), y, z, c)))
    outs += [count_block(n) for n in range(2, cols // 256)]
    tot = fq[x]
    for i in (1, 3, 2):
        arrive(landing(fx.at[i - 1], fx_r.at[i - 1]))
        tot = tot + fx[i - 1]
    first[...] = tot
    for cond, cp in sends:
        if cond is None:
            cp.wait_send()
        else:
            pl.when(cond)(cp.wait_send)
    for cp in outs:
        cp.wait()


def per_device(transition, emission, forward, beta_end, scales, tokens):
    rows, cols = transition.shape
    blk = cols // 4
    dma = pltpu.SemaphoreType.DMA
    vm = pltpu.VMEM
    hbm = pl.BlockSpec(memory_space=pl.ANY)
    vmem = pl.BlockSpec(memory_space=pltpu.VMEM)
    return pl.pallas_call(
        kernel,
        out_shape=(
            jax.ShapeDtypeStruct((rows, cols), F32),
            jax.ShapeDtypeStruct((B // 8, rows), F32),
        ),
        in_specs=[hbm, hbm, hbm, hbm, vmem, vmem],
        out_specs=(hbm, vmem),
        scratch_shapes=[
            vm((rows, cols), BF),
            vm((NY, emission.shape[0], blk), BF),
            vm((STEPS, B, rows), BF),
            vm((32, blk), BF),
            vm((rows, STEPS * B), BF),
            vm((STEPS, 8, 32, 128), F32),
            vm((STEPS, 8, 32, 128), F32),
            vm((8, 32, blk), BF),
            vm((7, 32, blk), BF),
            vm((8, 2, 32, blk), BF),
            vm((7, 2, 32, blk), BF),
            vm((2, 32, blk), BF),
            vm((2, 2, 32, blk), BF),
            vm((STEPS, 4, 2, 32, cols), BF),
            vm((2, 2, 2, 4, 16, rows), F32),
            vm((2, 2, 2, 4, 16, rows), BF),
            vm((2, 2, 4, 16, rows), BF),
            vm((2, 2, 4, 16, rows), BF),
            vm((2, 2, NX, NC, 16, rows), BF),
            vm((2, 4, 32, rows), F32),
            vm((4, 32, rows), F32),
            vm((4, 32, rows), F32),
            vm((3, 32, rows), F32),
            vm((rows, cols), F32),
            dma((4,)),
            dma((8,)),
            dma((3,)), dma((3,)),
            dma((7,)), dma((7,)),
            dma((7,)), dma((7,)),
            dma((7,)), dma((7,)),
            dma((1,)), dma((2,)),
            dma((3, 2, 3)), dma((3, 2, 3)),
            dma((2, 2)), dma((2, 2)),
            dma((2, 2, 4)), dma((2, 2, 8)),
            dma((2, 2, 7)), dma((2, 2, 4)),
            dma((1,)), dma((1,)),
            dma((3,)), dma((3,)),
        ],
        compiler_params=pltpu.CompilerParams(
            collective_id=0, has_side_effects=True, vmem_limit_bytes=48 * 1024 * 1024
        ),
        name="window",
    )(transition, emission, forward, beta_end, scales, tokens)


def solution(mesh):
    in_specs = (P("src", "dst"), P("src", "dst"), P(None, None, "src"), P(None, "dst"), P(), P())
    out_specs = (P("src", "dst"), P("dst", "src"))
    return jax.shard_map(
        per_device, mesh=mesh, in_specs=in_specs, out_specs=out_specs, check_vma=False
    )
```

time: 518 us -> 126 us (0.24)
  waiting for transfers between devices: 398 us -> 0 us
  Pallas kernels: 0 us -> 113 us
  blocking collectives: 61.7 us -> 0 us
  matrix products: 22 us -> 0 us
  between operations: 13.9 us -> 0.65 us
  other arithmetic: 6.79 us -> 0 us
    psum x2 -> x0, waiting for transfers between devices: 212 us -> none  [the longest x1 158 us: emitted_window(): lax.psum(local_rows(words, emission, first_word), 'src').astype(jnp.float32)]
    all_gather x2 -> x0, waiting for transfers between devices: 186 us -> none  [per_device(): lax.all_gather(summed.astype(jnp.bfloat16), 'src', axis=1, tiled=True)]
    pallas_call x0 -> x1, Pallas kernels: none -> 113 us  [per_device(): pl.pallas_call(kernel, out_shape=(jax.ShapeDtypeStruct((rows, cols), F32)...]
    psum x2 -> x0, blocking collectives: 61.7 us -> none  [per_device(): summed = lax.psum(partial_rows, 'dst')]
    dot_general x7 -> x0, matrix products: 22 us -> none  [the longest x3 14.7 us: per_device(): lax.dot_general(forward[step], weighted, (((0,), (0,)), ((), ())), prefer...]
    convert_element_type x3 -> x0, other arithmetic: 6.02 us -> none  [per_device(): weighted = (emitted.astype(jnp.float32) * message.astype(jnp.float32) / s...]
    unnamed x18 -> x14, local copies, waits for them, and re-layouts: 12.2 us -> 11.9 us
  transfers between devices with their start and end apart: 4 -> 0, of which waited for: 4 -> 0; matrix products, arithmetic and copies ran while one was open for 4% -> 0% of each run, Pallas kernels for 0% -> 0%
where the time goes in v1:
time: 126 us
  Pallas kernels  113 us (90%)
  local copies, waits for them, and re-layouts  11.9 us (9%)
    pallas_call x1, Pallas kernels, per_device(): pl.pallas_call(kernel, out_shape=(jax.ShapeDtypeStruct((rows, cols), F32)...  113 us
    unnamed x14, local copies, waits for them, and re-layouts  11.9 us

profile of v1, /device:TPU:1, one launch (start us, length us, event | category | flops | bytes accessed | tf_op | source)
XLA Modules:
  0.0 126.0 jit_solution(2101334915618981068)
XLA Ops:
  0.6 0.0 copy-start
  0.6 1.6 %copy-done = bf16[512,2048]{1,0:T(8,128)(2,1)S(1)} copy-done((bf16[512,2048]{1,0:T(8,128)(2,1)S(1)}, bf16[512,2048]{1,0:T(8,128)(2,1)}, u32[]{:S(2)}) %copy-start) | copy-done | bytes 2097176
  2.2 0.0 copy-start.1
  2.2 1.2 copy-done.1
  3.4 0.0 copy-start.2
  3.5 1.2 copy-done.2
  4.7 0.0 copy-start.3
  4.7 1.1 copy-done.3
  5.8 0.0 copy-start.4
  5.8 0.7 copy-done.4
  6.5 0.0 copy-start.5
  6.5 0.7 copy-done.5
  7.2 113.4 %window.1 = (f32[512,2048]{1,0:T(8,128)}, f32[32,512]{1,0:T(8,128)S(1)}) custom-call(bf16[512,2048]{1,0:T(8,128)(2,1)S(1)} %copy-done, bf16[256,2048]{1,0:T(8,128)(2,1)S(1)} %copy-done.1, bf16[3,256,512]{2,1,0:T(8,128)(2,1)S(1)} %copy-done.3, bf16[256,2048]{1,0:T(8,128)(2,1)S(1)} %copy-done.2, f32[3,256]{1,0:T(4,128)S(1)} %copy-done.4, s32[3,256]{1,0:T(4,128)S(1)} %copy-done.5), custom_call_target="tpu_custom_call" | custom-call | tf_op jit(solution)/shard_map/window/pallas_call | solution.py:318
  120.6 4.7 %copy.10 = f32[512,2048]{1,0:T(8,128)} copy(f32[512,2048]{1,0:T(8,128)} %get-tuple-element.4) | data formatting | bytes 8388608
  125.3 0.6 copy.11
Async XLA Ops:
  0.6 1.6 %copy-start = (bf16[512,2048]{1,0:T(8,128)(2,1)S(1)}, bf16[512,2048]{1,0:T(8,128)(2,1)}, u32[]{:S(2)}) copy-start(bf16[512,2048]{1,0:T(8,128)(2,1)} %trans.1) | copy-start | bytes 6291460
  2.2 1.2 copy-start.1
  3.4 1.2 copy-start.2
  4.7 1.1 copy-start.3
  5.8 0.7 copy-start.4
  6.5 0.7 copy-start.5

commit v2 on v0

v2 whole, which is shorter than its diff:
```python
import jax
import jax.numpy as jnp
from jax import lax
from jax.experimental import pallas as pl
from jax.experimental.pallas import tpu as pltpu
from jax.sharding import PartitionSpec as P

MESH = pl.DeviceIdType.MESH
NX, NY, NZ, NC = 4, 4, 8, 2
B = 256
STEPS = 3
NT = 4
BF = jnp.bfloat16
F32 = jnp.float32
FAR = (4, 3, 5, 2, 6, 1, 7)
NEAR = (1, 7, 2, 6, 3, 5, 4)


def dev(x, y, z, c):
    return (y * NZ + z, x * NC + c)


def kernel(
    trans, emis, forw, beta, scales_in, tokens_in,
    counts, first,
    scales, tokens, tv, tt, ev, fv, bv, ft, sc, tc, hot,
    x2, rz2, x10, rz10, em_s, em,
    w, own, pb, pr, qb, orx, fp, fx,
    l_sem, rdy,
    e_s, e_r, z2_s, z2_r, zw_s, zw_r, z10_s, z10_r, pm_s, pm_r,
    y_s, y_r, pp_s, pp_r, o_s, o_r, zz_s, zz_r, fx_s, fx_r,
):
    s = lax.axis_index("src")
    d = lax.axis_index("dst")
    y, z = s // NZ, s % NZ
    x, c = d // NC, d % NC
    sib = 1 - c
    words = emis.shape[0]
    cols = emis.shape[1]
    blk = cols // 4
    hb = blk // 2
    rows = trans.shape[0]
    yo = pl.multiple_of(y * blk, blk)
    oc = z // 4
    q = z % 4
    qo = pl.multiple_of(q * blk, blk)
    is_owner = c == oc

    def zp(i):
        return lax.rem(z + i, NZ)

    def yp(i):
        return lax.rem(y + i, NY)

    def xp(i):
        return lax.rem(x + i, NX)

    barrier = pltpu.get_barrier_semaphore()
    z_near = [dev(x, y, zp(i), c) for i in (1, NZ - 1)]
    x_near = [dev(xp(i), y, z, c) for i in (1, NX - 1)]
    peers = [dev(x, y, z, sib)] + [dev(x, yp(i), z, c) for i in range(1, NY)] + z_near + x_near

    def greet(sem, to):
        for p in to:
            pl.semaphore_signal(sem, inc=1, device_id=p, device_id_type=MESH)

    greet(barrier, peers)
    loads = [
        pltpu.make_async_copy(emis.at[:, pl.ds(yo, hb)], ev.at[0, y], l_sem.at[0]),
        pltpu.make_async_copy(
            emis.at[:, pl.ds(pl.multiple_of(y * blk + hb, hb), hb)], ev.at[1, y], l_sem.at[1]
        ),
        pltpu.make_async_copy(
            beta.at[pl.ds(pl.multiple_of(z * 32, 32), 32), pl.ds(yo, blk)], bv, l_sem.at[2]
        ),
        pltpu.make_async_copy(trans, tv, l_sem.at[3]),
        pltpu.make_async_copy(forw, fv, l_sem.at[4]),
        pltpu.make_async_copy(scales_in, scales, l_sem.at[5]),
        pltpu.make_async_copy(tokens_in, tokens, l_sem.at[6]),
    ]
    for cp in loads:
        cp.start()
    pl.semaphore_wait(barrier, len(peers))

    sends = []

    def remote(src, dst, ss, rs, to):
        return pltpu.make_async_remote_copy(
            src_ref=src, dst_ref=dst, send_sem=ss, recv_sem=rs, device_id=to, device_id_type=MESH
        )

    def send(cp, cond=None):
        if cond is None:
            cp.start()
        else:
            pl.when(cond)(cp.start)
        sends.append((cond, cp))

    here = dev(x, y, z, sib)

    def arrive(dst, rs, cond=None):
        cp = remote(dst, dst, rs, rs, here)
        if cond is None:
            cp.wait_recv()
        else:
            pl.when(cond)(cp.wait_recv)

    for h in range(2):
        for i in (2, 1, 3):
            yt = yp(i)
            send(
                remote(
                    emis.at[:, pl.ds(pl.multiple_of(yt * blk + h * hb, hb), hb)],
                    ev.at[h, y], e_s.at[h, i - 1], e_r.at[h, i - 1], dev(x, yt, z, c),
                )
            )

    for cp in loads[2:]:
        cp.wait()
    eye = lax.broadcasted_iota(jnp.int32, (B, B), 0) == lax.broadcasted_iota(jnp.int32, (B, B), 1)
    for k in (2, 1, 0):
        for src, dst in ((tokens[k : k + 1, :].astype(F32), tc), (scales[k : k + 1, :], sc)):
            col = jnp.sum(jnp.where(eye, jnp.broadcast_to(src, (B, B)), 0.0), axis=1, keepdims=True)
            dst[k] = jnp.broadcast_to(col, (B, 128)).reshape(16, 16, 128)
        tok = tc[k].reshape(B, 128)
        for j in range(NY):
            base = ((j * NZ + z) * words).astype(F32)
            for t in range(words // 128):
                lane = lax.broadcasted_iota(jnp.int32, (B, 128), 1).astype(F32) + (base + 128.0 * t)
                at = j * words + t * 128
                hot[k, :, at : at + 128] = jnp.where(tok == lane, 1.0, 0.0).astype(BF)
    for k in range(STEPS):
        ft[:, k * B : (k + 1) * B] = fv[k].astype(F32).T.astype(BF)

    greet(rdy.at[3], x_near)
    for j in range(3):
        greet(rdy.at[j], z_near)
        pl.semaphore_wait(rdy.at[j], 2)
    pl.semaphore_wait(rdy.at[3], 2)

    def lookup(k, h):
        return jnp.dot(
            hot[k], ev[h].reshape(NY * words, hb), preferred_element_type=F32
        ).astype(BF).reshape(8, 32, hb)

    for h in range(2):
        loads[h].wait()
        for i in (1, 3, 2):
            arrive(ev.at[h, yp(NY - i)], e_r.at[h, i - 1])
        x2[h] = lookup(2, h)
        for i in FAR:
            send(
                remote(
                    x2.at[h, zp(i)], rz2.at[h, i - 1], z2_s.at[h, i - 1], z2_r.at[h, i - 1],
                    dev(x, y, zp(i), c),
                )
            )
        part = pl.multiple_of((sib if h == 0 else c) * (rows // 2), rows // 2)
        for lo in range(0, cols, 512):
            tt[h, lo : lo + 512, :] = tv[pl.ds(part, rows // 2), lo : lo + 512].astype(F32).T.astype(BF)

    for kk in (1, 0):
        for h in range(2):
            x10[kk, :, :, h * hb : (h + 1) * hb] = lookup(kk, h)

    def scaled(value, k, g):
        den = sc[k, g]
        return value / jnp.concatenate([den] * (value.shape[-1] // 128), axis=1)

    for h in range(2):
        tot = x2[h, z].astype(F32)
        for i in NEAR:
            arrive(rz2.at[h, i - 1], z2_r.at[h, i - 1])
            tot = tot + rz2[h, i - 1].astype(F32)
        tot = tot * bv[:, h * hb : (h + 1) * hb].astype(F32)
        ho = pl.ds(pl.multiple_of(y * blk + h * hb, hb), hb)
        for u in range(2):
            w[2, z // 2, 2 * (z % 2) + u, :, ho] = scaled(
                tot[u * 16 : (u + 1) * 16], 2, 2 * z + u
            ).astype(BF)
        mine = w.at[2, z // 2, pl.ds(2 * (z % 2), 2), :, ho]
        for i in FAR:
            send(
                remote(mine, mine, zw_s.at[h, i - 1], zw_r.at[h, i - 1], dev(x, y, zp(i), c))
            )

    def spread(kk):
        for i in FAR:
            send(
                remote(
                    x10.at[kk, zp(i)], rz10.at[kk, i - 1], z10_s.at[kk, i - 1], z10_r.at[kk, i - 1],
                    dev(x, y, zp(i), c),
                )
            )

    spread(1)
    for h in range(2):
        ho = pl.ds(pl.multiple_of(y * blk + h * hb, hb), hb)
        for i in NEAR:
            zt = zp(NZ - i)
            arrive(w.at[2, zt // 2, pl.ds(2 * (zt % 2), 2), :, ho], zw_r.at[h, i - 1])
    def y_part(k, t, yt):
        if k == 2:
            return w.at[2, :, t, :, pl.ds(pl.multiple_of(yt * blk, blk), blk)]
        return w.at[k, yt, t]

    def y_send(k, t):
        part = y_part(k, t, y)
        for i in (2, 1, 3):
            send(remote(part, part, y_s.at[k, t, i - 1], y_r.at[k, t, i - 1], dev(x, yp(i), z, c)))

    for t in range(NT):
        y_send(2, t)
    spread(0)

    def wait_rows(k, t):
        for i in (1, 3, 2):
            arrive(y_part(k, t, yp(NY - i)), y_r.at[k, t, i - 1])

    def product(k, t, j):
        return jnp.dot(
            w[k, :, t].reshape(B // NT, cols), tt[j], preferred_element_type=F32
        ).reshape(4, 16, rows // 2)

    def rows_of(k, t):
        wait_rows(k + 1, t)
        pb[k, t] = product(k + 1, t, 0).astype(BF)
        send(remote(pb.at[k, t], pr.at[k, t], pp_s.at[k, t], pp_r.at[k, t], dev(x, y, z, sib)))
        own[k, t] = product(k + 1, t, 1)
        arrive(pr.at[k, t], pp_r.at[k, t])
        qb[k, t] = (own[k, t] + pr[k, t].astype(F32)).astype(BF)
        for r in range(NY):
            self_r = (x == y) & (y == r) & is_owner
            send(
                remote(
                    qb.at[k, t, r], orx.at[k, t, x, c], o_s.at[k, t, r], o_r.at[k, t, x * 2 + c],
                    dev(y, r, z, oc),
                ),
                jnp.logical_not(self_r),
            )

            @pl.when(self_r)
            def _():
                orx[k, t, x, c] = qb[k, t, r]

    pm_self = (y == z // 2) & (z == 4 * c + y)

    def tiles(kk):
        acc = x10[kk, z].astype(F32)
        for i in NEAR:
            arrive(rz10.at[kk, i - 1], z10_r.at[kk, i - 1])
            acc = acc + rz10[kk, i - 1].astype(F32)
        em_s[kk] = acc.astype(BF)
        send(
            remote(
                em_s.at[kk], em.at[kk, z % 2], pm_s.at[kk], pm_r.at[kk, z % 2],
                dev(x, z // 2, 4 * c + y, c),
            ),
            jnp.logical_not(pm_self),
        )

        @pl.when(pm_self)
        def _():
            em[kk, z % 2] = em_s[kk]

    def tiles_done(kk):
        for h in range(2):
            from_self = (y == q) & (z == 2 * y + h)
            arrive(em.at[kk, h], pm_r.at[kk, h], is_owner & jnp.logical_not(from_self))

    def owner(k, t):
        for j in range(8):
            from_self = (x == y) & (x * 2 + c == j)
            arrive(
                orx.at[k, t, j // 2, j % 2], o_r.at[k, t, j],
                is_owner & jnp.logical_not(from_self),
            )

        @pl.when(is_owner)
        def _():
            halves = []
            for cc in range(2):
                acc = orx[k, t, 0, cc].astype(F32)
                for xx in range(1, NX):
                    acc = acc + orx[k, t, xx, cc].astype(F32)
                halves.append(acc)
            msg = jnp.concatenate(halves, axis=1).astype(BF).astype(F32)
            lo = 16 * (t % 2)
            w[k, y, t, :, pl.ds(qo, blk)] = scaled(
                em[k, t // 2, lo : lo + 16].astype(F32) * msg, k, 4 * y + t
            ).astype(BF)

        tile = w.at[k, y, t, :, pl.ds(qo, blk)]
        for i in FAR:
            send(
                remote(tile, tile, zz_s.at[k, t, i - 1], zz_r.at[k, t, q], dev(x, y, zp(i), c)),
                is_owner,
            )

    def column(k, t):
        for j in range(4):
            arrive(w.at[k, y, t, :, j * blk : (j + 1) * blk], zz_r.at[k, t, j], z != 4 * c + j)
        y_send(k, t)

    def last(t):
        wait_rows(0, t)
        for j, half in ((0, sib), (1, c)):
            fp[t, :, :, pl.ds(pl.multiple_of(half * (rows // 2), rows // 2), rows // 2)] = product(
                0, t, j
            )
        to = t // 2
        u = t % 2
        for i in (2, 1, 3, 0):
            send(
                remote(
                    fp.at[t, xp(i)], fx.at[u, i, c], fx_s.at[t, i], fx_r.at[u, i, c],
                    dev(xp(i), y, z, to),
                ),
                c != to if i == 0 else None,
            )

    rows_of(1, 0)
    rows_of(1, 1)
    tiles(1)
    rows_of(1, 2)
    tiles_done(1)
    owner(1, 0)
    rows_of(1, 3)
    owner(1, 1)
    owner(1, 2)
    column(1, 0)
    owner(1, 3)
    column(1, 1)
    tiles(0)
    column(1, 2)
    rows_of(0, 0)
    column(1, 3)
    rows_of(0, 1)
    rows_of(0, 2)
    tiles_done(0)
    owner(0, 0)
    rows_of(0, 3)
    owner(0, 1)
    owner(0, 2)
    column(0, 0)
    owner(0, 3)
    column(0, 1)
    column(0, 2)
    last(0)
    column(0, 3)
    last(1)
    last(2)
    last(3)

    def count_block(n):
        lo = n * 256
        acc = jnp.dot(
            ft[...], w[:, :, :, :, lo : lo + 256].reshape(STEPS * B, 256), preferred_element_type=F32
        )
        counts[:, lo : lo + 256] = tv[:, lo : lo + 256].astype(F32) * acc * (32.0 / (STEPS * B))

    for n in range(cols // 256):
        count_block(n)
    for u in range(2):
        tot = fp[2 * c + u, x]
        for i, core in [(0, sib)] + [(i, j) for i in (1, 3, 2) for j in range(2)]:
            arrive(fx.at[u, i, core], fx_r.at[u, i, core])
            tot = tot + fx[u, i, core]
        first[u * 16 : (u + 1) * 16] = tot
    for cond, cp in sends:
        if cond is None:
            cp.wait_send()
        else:
            pl.when(cond)(cp.wait_send)


def per_device(*args):
    transition, emission = args[:2]
    rows, cols = transition.shape
    blk = cols // 4
    words = emission.shape[0]
    dma = pltpu.SemaphoreType.DMA
    vm = pltpu.VMEM
    hbm = pl.BlockSpec(memory_space=pltpu.HBM)
    vmem = pl.BlockSpec(memory_space=pltpu.VMEM)
    return pl.pallas_call(
        kernel,
        out_shape=(
            jax.ShapeDtypeStruct((rows, cols), F32),
            jax.ShapeDtypeStruct((B // 8, rows), F32),
        ),
        in_specs=[hbm] * 6,
        out_specs=(vmem, vmem),
        scratch_shapes=[
            vm((STEPS, B), F32),
            vm((STEPS, B), jnp.int32),
            vm((rows, cols), BF),
            vm((2, cols, rows // 2), BF),
            vm((2, NY, words, blk // 2), BF),
            vm((STEPS, B, rows), BF),
            vm((32, blk), BF),
            vm((rows, STEPS * B), BF),
            vm((STEPS, 16, 16, 128), F32),
            vm((STEPS, 16, 16, 128), F32),
            vm((STEPS, B, NY * words), BF),
            vm((2, 8, 32, blk // 2), BF),
            vm((2, 7, 32, blk // 2), BF),
            vm((2, 8, 32, blk), BF),
            vm((2, 7, 32, blk), BF),
            vm((2, 32, blk), BF),
            vm((2, 2, 32, blk), BF),
            vm((STEPS, 4, NT, 16, cols), BF),
            vm((2, NT, 4, 16, rows // 2), F32),
            vm((2, NT, 4, 16, rows // 2), BF),
            vm((2, NT, 4, 16, rows // 2), BF),
            vm((2, NT, 4, 16, rows // 2), BF),
            vm((2, NT, NX, NC, 16, rows // 2), BF),
            vm((NT, 4, 16, rows), F32),
            vm((2, NX, NC, 16, rows), F32),
            dma((7,)),
            pltpu.SemaphoreType.REGULAR((4,)),
            dma((2, 3)), dma((2, 3)),
            dma((2, 7)), dma((2, 7)),
            dma((2, 7)), dma((2, 7)),
            dma((2, 7)), dma((2, 7)),
            dma((2,)), dma((2, 2)),
            dma((3, NT, 3)), dma((3, NT, 3)),
            dma((2, NT)), dma((2, NT)),
            dma((2, NT, 4)), dma((2, NT, 8)),
            dma((2, NT, 7)), dma((2, NT, 4)),
            dma((NT, NX)), dma((2, NX, NC)),
        ],
        compiler_params=pltpu.CompilerParams(
            collective_id=0, has_side_effects=True, vmem_limit_bytes=30 * 1024 * 1024
        ),
        name="window",
    )(*(pltpu.with_memory_space_constraint(a, pltpu.HBM) for a in args))


def solution(mesh):
    in_specs = (P("src", "dst"), P("src", "dst"), P(None, None, "src"), P(None, "dst"), P(), P())
    out_specs = (P("src", "dst"), P("dst", "src"))
    return jax.shard_map(
        per_device, mesh=mesh, in_specs=in_specs, out_specs=out_specs, check_vma=False
    )
```

time: 518 us -> 98.4 us (0.19)
  waiting for transfers between devices: 398 us -> 0 us
  Pallas kernels: 0 us -> 95.1 us
  blocking collectives: 61.7 us -> 0 us
  matrix products: 22 us -> 0 us
  between operations: 13.9 us -> 0.64 us
  local copies, waits for them, and re-layouts: 13.7 us -> 2.64 us
  other arithmetic: 6.79 us -> 0 us
    psum x2 -> x0, waiting for transfers between devices: 212 us -> none  [the longest x1 158 us: emitted_window(): lax.psum(local_rows(words, emission, first_word), 'src').astype(jnp.float32)]
    all_gather x2 -> x0, waiting for transfers between devices: 186 us -> none  [per_device(): lax.all_gather(summed.astype(jnp.bfloat16), 'src', axis=1, tiled=True)]
    pallas_call x0 -> x1, Pallas kernels: none -> 95.1 us  [per_device(): pl.pallas_call(kernel, out_shape=(jax.ShapeDtypeStruct((rows, cols), F32)...]
    psum x2 -> x0, blocking collectives: 61.7 us -> none  [per_device(): summed = lax.psum(partial_rows, 'dst')]
    dot_general x7 -> x0, matrix products: 22 us -> none  [the longest x3 14.7 us: per_device(): lax.dot_general(forward[step], weighted, (((0,), (0,)), ((), ())), prefer...]
    unnamed x18 -> x2, local copies, waits for them, and re-layouts: 12.2 us -> 2.64 us
    convert_element_type x3 -> x0, other arithmetic: 6.02 us -> none  [per_device(): weighted = (emitted.astype(jnp.float32) * message.astype(jnp.float32) / s...]
  transfers between devices with their start and end apart: 4 -> 0, of which waited for: 4 -> 0; matrix products, arithmetic and copies ran while one was open for 4% -> 0% of each run, Pallas kernels for 0% -> 0%
where the time goes in v2:
time: 98.4 us
  Pallas kernels  95.1 us (97%)
  local copies, waits for them, and re-layouts  2.64 us (3%)
    pallas_call x1, Pallas kernels, per_device(): pl.pallas_call(kernel, out_shape=(jax.ShapeDtypeStruct((rows, cols), F32)...  95.1 us
    unnamed x2, local copies, waits for them, and re-layouts  2.64 us

profile of v2, /device:TPU:1, one launch (start us, length us, event | category | flops | bytes accessed | tf_op | source)
XLA Modules:
  0.0 98.4 jit_solution(15550154663020045906)
XLA Ops:
  0.6 95.1 %window.1 = (f32[512,2048]{1,0:T(8,128)S(1)}, f32[32,512]{1,0:T(8,128)S(1)}) custom-call(bf16[512,2048]{1,0:T(8,128)(2,1)} %trans.1, bf16[256,2048]{1,0:T(8,128)(2,1)} %emis.1, bf16[3,256,512]{2,1,0:T(8,128)(2,1)} %forw.1, bf16[256,2048]{1,0:T(8,128)(2,1)} %beta.1, f32[3,256]{1,0:T(4,128)} %scales_in.1, s32[3,256]{1,0:T(4,128)} %tokens_in.1), custom_call_target="tpu_custom_call" | custom-call | tf_op jit(solution)/shard_map/window/pallas_call | solution.py:386
  95.7 2.0 %copy.10 = f32[512,2048]{1,0:T(8,128)} copy(f32[512,2048]{1,0:T(8,128)S(1)} %get-tuple-element.4) | data formatting | bytes 8388608
  97.7 0.6 copy.11

commit v3 on v2

--- a/solution.py
+++ b/solution.py
@@ -28,7 +28,7 @@
     w, own, pb, pr, qb, orx, fp, fx,
     l_sem, rdy,
     e_s, e_r, z2_s, z2_r, zw_s, zw_r, z10_s, z10_r, pm_s, pm_r,
-    y_s, y_r, pp_s, pp_r, o_s, o_r, zz_s, zz_r, fx_s, fx_r,
+    ya_s, ya_r, y_s, y_r, pp_s, pp_r, o_s, o_r, zz_s, zz_r, fx_s, fx_r,
 ):
     s = lax.axis_index("src")
     d = lax.axis_index("dst")
@@ -82,38 +82,43 @@
         cp.start()
     pl.semaphore_wait(barrier, len(peers))
 
-    sends = []
-
-    def remote(src, dst, ss, rs, to):
-        return pltpu.make_async_remote_copy(
+    sent = []
+
+    def send(src, dst, ss, rs, to, cond=None):
+        cp = pltpu.make_async_remote_copy(
             src_ref=src, dst_ref=dst, send_sem=ss, recv_sem=rs, device_id=to, device_id_type=MESH
         )
-
-    def send(cp, cond=None):
         if cond is None:
             cp.start()
         else:
             pl.when(cond)(cp.start)
-        sends.append((cond, cp))
+
+    def sent_all(size, sem, cond=None):
+        sent.append((cond, size, sem))
 
     here = dev(x, y, z, sib)
 
-    def arrive(dst, rs, cond=None):
-        cp = remote(dst, dst, rs, rs, here)
+    def whole(size, sem):
+        return pltpu.make_async_remote_copy(
+            src_ref=size, dst_ref=size, send_sem=sem, recv_sem=sem,
+            device_id=here, device_id_type=MESH,
+        )
+
+    def arrive(size, sem, cond=None):
+        wait = whole(size, sem).wait_recv
         if cond is None:
-            cp.wait_recv()
+            wait()
         else:
-            pl.when(cond)(cp.wait_recv)
+            pl.when(cond)(wait)
 
     for h in range(2):
         for i in (2, 1, 3):
             yt = yp(i)
             send(
-                remote(
-                    emis.at[:, pl.ds(pl.multiple_of(yt * blk + h * hb, hb), hb)],
-                    ev.at[h, y], e_s.at[h, i - 1], e_r.at[h, i - 1], dev(x, yt, z, c),
-                )
+                emis.at[:, pl.ds(pl.multiple_of(yt * blk + h * hb, hb), hb)],
+                ev.at[h, y], e_s.at[h], e_r.at[h], dev(x, yt, z, c),
             )
+        sent_all(ev.at[h, 0:3], e_s.at[h])
 
     for cp in loads[2:]:
         cp.wait()
@@ -145,16 +150,11 @@
 
     for h in range(2):
         loads[h].wait()
-        for i in (1, 3, 2):
-            arrive(ev.at[h, yp(NY - i)], e_r.at[h, i - 1])
+        arrive(ev.at[h, 0:3], e_r.at[h])
         x2[h] = lookup(2, h)
         for i in FAR:
-            send(
-                remote(
-                    x2.at[h, zp(i)], rz2.at[h, i - 1], z2_s.at[h, i - 1], z2_r.at[h, i - 1],
-                    dev(x, y, zp(i), c),
-                )
-            )
+            send(x2.at[h, zp(i)], rz2.at[h, i - 1], z2_s.at[h], z2_r.at[h], dev(x, y, zp(i), c))
+        sent_all(rz2.at[h], z2_s.at[h])
         part = pl.multiple_of((sib if h == 0 else c) * (rows // 2), rows // 2)
         for lo in range(0, cols, 512):
             tt[h, lo : lo + 512, :] = tv[pl.ds(part, rows // 2), lo : lo + 512].astype(F32).T.astype(BF)
@@ -169,8 +169,8 @@
 
     for h in range(2):
         tot = x2[h, z].astype(F32)
+        arrive(rz2.at[h], z2_r.at[h])
         for i in NEAR:
-            arrive(rz2.at[h, i - 1], z2_r.at[h, i - 1])
             tot = tot + rz2[h, i - 1].astype(F32)
         tot = tot * bv[:, h * hb : (h + 1) * hb].astype(F32)
         ho = pl.ds(pl.multiple_of(y * blk + h * hb, hb), hb)
@@ -180,84 +180,94 @@
             ).astype(BF)
         mine = w.at[2, z // 2, pl.ds(2 * (z % 2), 2), :, ho]
         for i in FAR:
-            send(
-                remote(mine, mine, zw_s.at[h, i - 1], zw_r.at[h, i - 1], dev(x, y, zp(i), c))
-            )
+            send(mine, mine, zw_s.at[h], zw_r.at[h], dev(x, y, zp(i), c))
+        sent_all(rz2.at[h], zw_s.at[h])
 
     def spread(kk):
         for i in FAR:
             send(
-                remote(
-                    x10.at[kk, zp(i)], rz10.at[kk, i - 1], z10_s.at[kk, i - 1], z10_r.at[kk, i - 1],
-                    dev(x, y, zp(i), c),
-                )
+                x10.at[kk, zp(i)], rz10.at[kk, i - 1], z10_s.at[kk], z10_r.at[kk],
+                dev(x, y, zp(i), c),
             )
+        sent_all(rz10.at[kk], z10_s.at[kk])
 
     spread(1)
+    three_a = w.at[2, 0:3, :, :, 0 : 4 * hb]
     for h in range(2):
         ho = pl.ds(pl.multiple_of(y * blk + h * hb, hb), hb)
-        for i in NEAR:
-            zt = zp(NZ - i)
-            arrive(w.at[2, zt // 2, pl.ds(2 * (zt % 2), 2), :, ho], zw_r.at[h, i - 1])
+        arrive(rz2.at[h], zw_r.at[h])
+        if h == 0:
+            part = w.at[2, :, :, :, ho]
+            for i in (2, 1, 3):
+                send(part, part, ya_s.at[0], ya_r.at[0], dev(x, yp(i), z, c))
+            sent_all(three_a, ya_s.at[0])
     def y_part(k, t, yt):
         if k == 2:
-            return w.at[2, :, t, :, pl.ds(pl.multiple_of(yt * blk, blk), blk)]
+            return w.at[2, :, t, :, pl.ds(pl.multiple_of(yt * blk + hb, hb), hb)]
         return w.at[k, yt, t]
+
+    def y_three(k, t):
+        return w.at[2, 0:3, t, :, 0 : 4 * hb] if k == 2 else w.at[k, 0:3, t]
 
     def y_send(k, t):
         part = y_part(k, t, y)
         for i in (2, 1, 3):
-            send(remote(part, part, y_s.at[k, t, i - 1], y_r.at[k, t, i - 1], dev(x, yp(i), z, c)))
+            send(part, part, y_s.at[k, t], y_r.at[k, t], dev(x, yp(i), z, c))
+        sent_all(y_three(k, t), y_s.at[k, t])
 
     for t in range(NT):
         y_send(2, t)
     spread(0)
 
     def wait_rows(k, t):
-        for i in (1, 3, 2):
-            arrive(y_part(k, t, yp(NY - i)), y_r.at[k, t, i - 1])
+        if k == 2 and t == 0:
+            arrive(three_a, ya_r.at[0])
+        arrive(y_three(k, t), y_r.at[k, t])
 
     def product(k, t, j):
         return jnp.dot(
             w[k, :, t].reshape(B // NT, cols), tt[j], preferred_element_type=F32
         ).reshape(4, 16, rows // 2)
 
-    def rows_of(k, t):
+    own_part = (x == y) & is_owner
+
+    def rows_of(k, t, meanwhile=None):
         wait_rows(k + 1, t)
         pb[k, t] = product(k + 1, t, 0).astype(BF)
-        send(remote(pb.at[k, t], pr.at[k, t], pp_s.at[k, t], pp_r.at[k, t], dev(x, y, z, sib)))
+        send(pb.at[k, t], pr.at[k, t], pp_s.at[k, t], pp_r.at[k, t], dev(x, y, z, sib))
+        sent_all(pb.at[k, t], pp_s.at[k, t])
         own[k, t] = product(k + 1, t, 1)
+        if meanwhile is not None:
+            meanwhile()
         arrive(pr.at[k, t], pp_r.at[k, t])
         qb[k, t] = (own[k, t] + pr[k, t].astype(F32)).astype(BF)
         for r in range(NY):
             self_r = (x == y) & (y == r) & is_owner
             send(
-                remote(
-                    qb.at[k, t, r], orx.at[k, t, x, c], o_s.at[k, t, r], o_r.at[k, t, x * 2 + c],
-                    dev(y, r, z, oc),
-                ),
-                jnp.logical_not(self_r),
+                qb.at[k, t, r], orx.at[k, t, x * 2 + c], o_s.at[k, t], o_r.at[k, t],
+                dev(y, r, z, oc), jnp.logical_not(self_r),
             )
 
             @pl.when(self_r)
             def _():
-                orx[k, t, x, c] = qb[k, t, r]
+                orx[k, t, x * 2 + c] = qb[k, t, r]
+
+        sent_all(qb.at[k, t, 0:3], o_s.at[k, t], own_part)
+        sent_all(qb.at[k, t], o_s.at[k, t], jnp.logical_not(own_part))
 
     pm_self = (y == z // 2) & (z == 4 * c + y)
 
     def tiles(kk):
         acc = x10[kk, z].astype(F32)
+        arrive(rz10.at[kk], z10_r.at[kk])
         for i in NEAR:
-            arrive(rz10.at[kk, i - 1], z10_r.at[kk, i - 1])
             acc = acc + rz10[kk, i - 1].astype(F32)
         em_s[kk] = acc.astype(BF)
         send(
-            remote(
-                em_s.at[kk], em.at[kk, z % 2], pm_s.at[kk], pm_r.at[kk, z % 2],
-                dev(x, z // 2, 4 * c + y, c),
-            ),
-            jnp.logical_not(pm_self),
+            em_s.at[kk], em.at[kk, z % 2], pm_s.at[kk], pm_r.at[kk, z % 2],
+            dev(x, z // 2, 4 * c + y, c), jnp.logical_not(pm_self),
         )
+        sent_all(em_s.at[kk], pm_s.at[kk], jnp.logical_not(pm_self))
 
         @pl.when(pm_self)
         def _():
@@ -269,20 +279,16 @@
             arrive(em.at[kk, h], pm_r.at[kk, h], is_owner & jnp.logical_not(from_self))
 
     def owner(k, t):
-        for j in range(8):
-            from_self = (x == y) & (x * 2 + c == j)
-            arrive(
-                orx.at[k, t, j // 2, j % 2], o_r.at[k, t, j],
-                is_owner & jnp.logical_not(from_self),
-            )
+        arrive(orx.at[k, t, 0:7], o_r.at[k, t], own_part)
+        arrive(orx.at[k, t], o_r.at[k, t], is_owner & jnp.logical_not(own_part))
 
         @pl.when(is_owner)
         def _():
             halves = []
             for cc in range(2):
-                acc = orx[k, t, 0, cc].astype(F32)
+                acc = orx[k, t, cc].astype(F32)
                 for xx in range(1, NX):
-                    acc = acc + orx[k, t, xx, cc].astype(F32)
+                    acc = acc + orx[k, t, 2 * xx + cc].astype(F32)
                 halves.append(acc)
             msg = jnp.concatenate(halves, axis=1).astype(BF).astype(F32)
             lo = 16 * (t % 2)
@@ -292,14 +298,12 @@
 
         tile = w.at[k, y, t, :, pl.ds(qo, blk)]
         for i in FAR:
-            send(
-                remote(tile, tile, zz_s.at[k, t, i - 1], zz_r.at[k, t, q], dev(x, y, zp(i), c)),
-                is_owner,
-            )
+            send(tile, tile, zz_s.at[k, t], zz_r.at[k, t], dev(x, y, zp(i), c), is_owner)
+        sent_all(rz2.at[0], zz_s.at[k, t], is_owner)
 
     def column(k, t):
-        for j in range(4):
-            arrive(w.at[k, y, t, :, j * blk : (j + 1) * blk], zz_r.at[k, t, j], z != 4 * c + j)
+        arrive(w.at[k, y, t, :, 0 : 3 * blk], zz_r.at[k, t], is_owner)
+        arrive(w.at[k, y, t], zz_r.at[k, t], jnp.logical_not(is_owner))
         y_send(k, t)
 
     def last(t):
@@ -312,16 +316,14 @@
         u = t % 2
         for i in (2, 1, 3, 0):
             send(
-                remote(
-                    fp.at[t, xp(i)], fx.at[u, i, c], fx_s.at[t, i], fx_r.at[u, i, c],
-                    dev(xp(i), y, z, to),
-                ),
-                c != to if i == 0 else None,
+                fp.at[t, xp(i)], fx.at[u, 2 * i + c], fx_s.at[t], fx_r.at[u],
+                dev(xp(i), y, z, to), c != to if i == 0 else None,
             )
-
-    rows_of(1, 0)
+        sent_all(fp.at[t], fx_s.at[t], c != to)
+        sent_all(fp.at[t, 0:3], fx_s.at[t], c == to)
+
+    rows_of(1, 0, lambda: tiles(1))
     rows_of(1, 1)
-    tiles(1)
     rows_of(1, 2)
     tiles_done(1)
     owner(1, 0)
@@ -363,15 +365,16 @@
         count_block(n)
     for u in range(2):
         tot = fp[2 * c + u, x]
-        for i, core in [(0, sib)] + [(i, j) for i in (1, 3, 2) for j in range(2)]:
-            arrive(fx.at[u, i, core], fx_r.at[u, i, core])
-            tot = tot + fx[u, i, core]
+        arrive(fx.at[u, 0:7], fx_r.at[u])
+        for j in [sib] + list(range(2, 8)):
+            tot = tot + fx[u, j]
         first[u * 16 : (u + 1) * 16] = tot
-    for cond, cp in sends:
+    for cond, size, sem in sent:
+        wait = whole(size, sem).wait_send
         if cond is None:
-            cp.wait_send()
+            wait()
         else:
-            pl.when(cond)(cp.wait_send)
+            pl.when(cond)(wait)
 
 
 def per_device(*args):
@@ -414,21 +417,22 @@
             vm((2, NT, 4, 16, rows // 2), BF),
             vm((2, NT, 4, 16, rows // 2), BF),
             vm((2, NT, 4, 16, rows // 2), BF),
-            vm((2, NT, NX, NC, 16, rows // 2), BF),
+            vm((2, NT, NX * NC, 16, rows // 2), BF),
             vm((NT, 4, 16, rows), F32),
-            vm((2, NX, NC, 16, rows), F32),
+            vm((2, NX * NC, 16, rows), F32),
             dma((7,)),
             pltpu.SemaphoreType.REGULAR((4,)),
-            dma((2, 3)), dma((2, 3)),
-            dma((2, 7)), dma((2, 7)),
-            dma((2, 7)), dma((2, 7)),
-            dma((2, 7)), dma((2, 7)),
+            dma((2,)), dma((2,)),
+            dma((2,)), dma((2,)),
+            dma((2,)), dma((2,)),
+            dma((2,)), dma((2,)),
             dma((2,)), dma((2, 2)),
-            dma((3, NT, 3)), dma((3, NT, 3)),
+            dma((1,)), dma((1,)),
+            dma((3, NT)), dma((3, NT)),
             dma((2, NT)), dma((2, NT)),
-            dma((2, NT, 4)), dma((2, NT, 8)),
-            dma((2, NT, 7)), dma((2, NT, 4)),
-            dma((NT, NX)), dma((2, NX, NC)),
+            dma((2, NT)), dma((2, NT)),
+            dma((2, NT)), dma((2, NT)),
+            dma((NT,)), dma((2,)),
         ],
         compiler_params=pltpu.CompilerParams(
             collective_id=0, has_side_effects=True, vmem_limit_bytes=30 * 1024 * 1024

time: 98.4 us -> 93.8 us (0.953)
  Pallas kernels: 95.1 us -> 90.4 us
    pallas_call x1, Pallas kernels: 95.1 us -> 90.4 us  [per_device(): pl.pallas_call(kernel, out_shape=(jax.ShapeDtypeStruct((rows, cols), F32)...]
where the time goes in v3:
time: 93.8 us; the launch traced here: 93.7 us
  Pallas kernels  90.4 us (96%)
  local copies, waits for them, and re-layouts  2.64 us (3%)
    pallas_call x1, Pallas kernels, per_device(): pl.pallas_call(kernel, out_shape=(jax.ShapeDtypeStruct((rows, cols), F32)...  90.4 us
    unnamed x2, local copies, waits for them, and re-layouts  2.64 us

profile of v3, /device:TPU:1, one launch (start us, length us, event | category | flops | bytes accessed | tf_op | source)
XLA Modules:
  0.0 93.7 jit_solution(16107862794370279849)
XLA Ops:
  0.6 90.4 %window.1 = (f32[512,2048]{1,0:T(8,128)S(1)}, f32[32,512]{1,0:T(8,128)S(1)}) custom-call(bf16[512,2048]{1,0:T(8,128)(2,1)} %trans.1, bf16[256,2048]{1,0:T(8,128)(2,1)} %emis.1, bf16[3,256,512]{2,1,0:T(8,128)(2,1)} %forw.1, bf16[256,2048]{1,0:T(8,128)(2,1)} %beta.1, f32[3,256]{1,0:T(4,128)} %scales_in.1, s32[3,256]{1,0:T(4,128)} %tokens_in.1), custom_call_target="tpu_custom_call" | custom-call | tf_op jit(solution)/shard_map/window/pallas_call | solution.py:389
  91.1 2.0 %copy.10 = f32[512,2048]{1,0:T(8,128)} copy(f32[512,2048]{1,0:T(8,128)S(1)} %get-tuple-element.4) | data formatting | bytes 8388608
  93.1 0.6 copy.11

commit v4 on v3

--- a/solution.py
+++ b/solution.py
@@ -23,11 +23,11 @@
 def kernel(
     trans, emis, forw, beta, scales_in, tokens_in,
     counts, first,
-    scales, tokens, tv, tt, ev, fv, bv, ft, sc, tc, hot,
+    scales, tokens, tv, tt, ev, fv, bv, ft, sc, hot, eb, xb, rzb, sb, ryb,
     x2, rz2, x10, rz10, em_s, em,
     w, own, pb, pr, qb, orx, fp, fx,
     l_sem, rdy,
-    e_s, e_r, z2_s, z2_r, zw_s, zw_r, z10_s, z10_r, pm_s, pm_r,
+    e_s, e_r, zb_s, zb_r, yb_s, yb_r, z2_s, z2_r, zw_s, zw_r, z10_s, z10_r, pm_s, pm_r,
     ya_s, ya_r, y_s, y_r, pp_s, pp_r, o_s, o_r, zz_s, zz_r, fx_s, fx_r,
 ):
     s = lax.axis_index("src")
@@ -39,6 +39,7 @@
     cols = emis.shape[1]
     blk = cols // 4
     hb = blk // 2
+    qb_ = blk // 4
     rows = trans.shape[0]
     yo = pl.multiple_of(y * blk, blk)
     oc = z // 4
@@ -78,7 +79,13 @@
         pltpu.make_async_copy(scales_in, scales, l_sem.at[5]),
         pltpu.make_async_copy(tokens_in, tokens, l_sem.at[6]),
     ]
-    for cp in loads:
+    corner = [
+        pltpu.make_async_copy(
+            emis.at[:, j * blk + hb + qb_ : (j + 1) * blk], eb.at[j], l_sem.at[7 + j]
+        )
+        for j in range(NY)
+    ]
+    for cp in loads[-1:] + corner + loads[:-1]:
         cp.start()
     pl.semaphore_wait(barrier, len(peers))
 
@@ -111,67 +118,105 @@
         else:
             pl.when(cond)(wait)
 
-    for h in range(2):
+    for h, lo, at, size in ((0, 0, 0, hb), (1, hb, 0, qb_), (2, hb + qb_, qb_, qb_)):
+        dst = ev.at[min(h, 1), y, :, at : at + size]
         for i in (2, 1, 3):
             yt = yp(i)
             send(
-                emis.at[:, pl.ds(pl.multiple_of(yt * blk + h * hb, hb), hb)],
-                ev.at[h, y], e_s.at[h], e_r.at[h], dev(x, yt, z, c),
+                emis.at[:, pl.ds(pl.multiple_of(yt * blk + lo, qb_), size)],
+                dst, e_s.at[h], e_r.at[h], dev(x, yt, z, c),
             )
-        sent_all(ev.at[h, 0:3], e_s.at[h])
-
-    for cp in loads[2:]:
-        cp.wait()
+        sent_all(ev.at[0, 0:3, :, 0:size], e_s.at[h])
+
     eye = lax.broadcasted_iota(jnp.int32, (B, B), 0) == lax.broadcasted_iota(jnp.int32, (B, B), 1)
-    for k in (2, 1, 0):
-        for src, dst in ((tokens[k : k + 1, :].astype(F32), tc), (scales[k : k + 1, :], sc)):
-            col = jnp.sum(jnp.where(eye, jnp.broadcast_to(src, (B, B)), 0.0), axis=1, keepdims=True)
-            dst[k] = jnp.broadcast_to(col, (B, 128)).reshape(16, 16, 128)
-        tok = tc[k].reshape(B, 128)
+
+    def as_column(row):
+        col = jnp.sum(jnp.where(eye, jnp.broadcast_to(row, (B, B)), 0.0), axis=1, keepdims=True)
+        return jnp.broadcast_to(col, (B, 128))
+
+    def hot_rows(k):
+        tok = as_column(tokens[k : k + 1, :].astype(F32))
         for j in range(NY):
             base = ((j * NZ + z) * words).astype(F32)
             for t in range(words // 128):
                 lane = lax.broadcasted_iota(jnp.int32, (B, 128), 1).astype(F32) + (base + 128.0 * t)
                 at = j * words + t * 128
                 hot[k, :, at : at + 128] = jnp.where(tok == lane, 1.0, 0.0).astype(BF)
-    for k in range(STEPS):
-        ft[:, k * B : (k + 1) * B] = fv[k].astype(F32).T.astype(BF)
-
-    greet(rdy.at[3], x_near)
+
+    loads[6].wait()
+    hot_rows(2)
+    for cp in corner:
+        cp.wait()
+    mine_hot = hot[2, :, pl.ds(pl.multiple_of(y * words, words), words)]
+    for j in range(NY):
+        xb[:, j] = (
+            jnp.dot(mine_hot, eb[j], preferred_element_type=F32).astype(BF).reshape(8, 32, qb_)
+        )
     for j in range(3):
         greet(rdy.at[j], z_near)
         pl.semaphore_wait(rdy.at[j], 2)
+    for i in FAR:
+        send(xb.at[zp(i)], rzb.at[i - 1], zb_s.at[0], zb_r.at[0], dev(x, y, zp(i), c))
+    sent_all(rzb, zb_s.at[0])
+
+    for cp in loads[2:6]:
+        cp.wait()
+    for k in (2, 1, 0):
+        sc[k] = as_column(scales[k : k + 1, :]).reshape(16, 16, 128)
+        if k < 2:
+            hot_rows(k)
+    for k in range(STEPS):
+        ft[:, k * B : (k + 1) * B] = fv[k].astype(F32).T.astype(BF)
+    greet(rdy.at[3], x_near)
     pl.semaphore_wait(rdy.at[3], 2)
 
-    def lookup(k, h):
+    def lookup(k, h, size):
         return jnp.dot(
-            hot[k], ev[h].reshape(NY * words, hb), preferred_element_type=F32
-        ).astype(BF).reshape(8, 32, hb)
-
-    for h in range(2):
+            hot[k], ev[h, :, :, 0:size].reshape(NY * words, size), preferred_element_type=F32
+        ).astype(BF).reshape(8, 32, size)
+
+    for h, size in ((0, hb), (1, qb_)):
         loads[h].wait()
-        arrive(ev.at[h, 0:3], e_r.at[h])
-        x2[h] = lookup(2, h)
+        arrive(ev.at[0, 0:3, :, 0:size], e_r.at[h])
+        x2[h, :, :, 0:size] = lookup(2, h, size)
         for i in FAR:
-            send(x2.at[h, zp(i)], rz2.at[h, i - 1], z2_s.at[h], z2_r.at[h], dev(x, y, zp(i), c))
-        sent_all(rz2.at[h], z2_s.at[h])
+            send(
+                x2.at[h, zp(i), :, 0:size], rz2.at[h, i - 1, :, 0:size], z2_s.at[h], z2_r.at[h],
+                dev(x, y, zp(i), c),
+            )
+        sent_all(rz2.at[h, :, :, 0:size], z2_s.at[h])
         part = pl.multiple_of((sib if h == 0 else c) * (rows // 2), rows // 2)
         for lo in range(0, cols, 512):
             tt[h, lo : lo + 512, :] = tv[pl.ds(part, rows // 2), lo : lo + 512].astype(F32).T.astype(BF)
-
+    arrive(rzb, zb_r.at[0])
+    tot = xb[z].astype(F32)
+    for i in range(7):
+        tot = tot + rzb[i].astype(F32)
+    sb[...] = tot.astype(BF)
+    for i in (2, 1, 3):
+        send(sb.at[yp(i)], ryb.at[i - 1], yb_s.at[0], yb_r.at[0], dev(x, yp(i), z, c))
+    sent_all(ryb, yb_s.at[0])
+    arrive(ev.at[0, 0:3, :, 0:qb_], e_r.at[2])
     for kk in (1, 0):
         for h in range(2):
-            x10[kk, :, :, h * hb : (h + 1) * hb] = lookup(kk, h)
+            x10[kk, :, :, h * hb : (h + 1) * hb] = lookup(kk, h, hb)
 
     def scaled(value, k, g):
         den = sc[k, g]
         return value / jnp.concatenate([den] * (value.shape[-1] // 128), axis=1)
 
     for h in range(2):
-        tot = x2[h, z].astype(F32)
-        arrive(rz2.at[h], z2_r.at[h])
+        size = (hb, qb_)[h]
+        tot = x2[h, z, :, 0:size].astype(F32)
+        arrive(rz2.at[h, :, :, 0:size], z2_r.at[h])
         for i in NEAR:
-            tot = tot + rz2[h, i - 1].astype(F32)
+            tot = tot + rz2[h, i - 1, :, 0:size].astype(F32)
+        if h == 1:
+            arrive(ryb, yb_r.at[0])
+            rest = sb[y].astype(F32)
+            for i in range(3):
+                rest = rest + ryb[i].astype(F32)
+            tot = jnp.concatenate([tot, rest], axis=1)
         tot = tot * bv[:, h * hb : (h + 1) * hb].astype(F32)
         ho = pl.ds(pl.multiple_of(y * blk + h * hb, hb), hb)
         for u in range(2):
@@ -231,14 +276,15 @@
 
     own_part = (x == y) & is_owner
 
-    def rows_of(k, t, meanwhile=None):
+    def partial_sums(k, t):
         wait_rows(k + 1, t)
-        pb[k, t] = product(k + 1, t, 0).astype(BF)
+        theirs, ours = product(k + 1, t, 0), product(k + 1, t, 1)
+        pb[k, t] = theirs.astype(BF)
+        own[k, t] = ours
         send(pb.at[k, t], pr.at[k, t], pp_s.at[k, t], pp_r.at[k, t], dev(x, y, z, sib))
         sent_all(pb.at[k, t], pp_s.at[k, t])
-        own[k, t] = product(k + 1, t, 1)
-        if meanwhile is not None:
-            meanwhile()
+
+    def pair_sums(k, t):
         arrive(pr.at[k, t], pp_r.at[k, t])
         qb[k, t] = (own[k, t] + pr[k, t].astype(F32)).astype(BF)
         for r in range(NY):
@@ -322,12 +368,17 @@
         sent_all(fp.at[t], fx_s.at[t], c != to)
         sent_all(fp.at[t, 0:3], fx_s.at[t], c == to)
 
-    rows_of(1, 0, lambda: tiles(1))
-    rows_of(1, 1)
-    rows_of(1, 2)
+    partial_sums(1, 0)
+    tiles(1)
+    pair_sums(1, 0)
+    partial_sums(1, 1)
+    partial_sums(1, 2)
+    pair_sums(1, 1)
+    partial_sums(1, 3)
+    pair_sums(1, 2)
+    pair_sums(1, 3)
     tiles_done(1)
     owner(1, 0)
-    rows_of(1, 3)
     owner(1, 1)
     owner(1, 2)
     column(1, 0)
@@ -335,13 +386,17 @@
     column(1, 1)
     tiles(0)
     column(1, 2)
-    rows_of(0, 0)
+    partial_sums(0, 0)
+    pair_sums(0, 0)
     column(1, 3)
-    rows_of(0, 1)
-    rows_of(0, 2)
+    partial_sums(0, 1)
+    pair_sums(0, 1)
+    partial_sums(0, 2)
+    pair_sums(0, 2)
     tiles_done(0)
     owner(0, 0)
-    rows_of(0, 3)
+    partial_sums(0, 3)
+    pair_sums(0, 3)
     owner(0, 1)
     owner(0, 2)
     column(0, 0)
@@ -404,8 +459,12 @@
             vm((32, blk), BF),
             vm((rows, STEPS * B), BF),
             vm((STEPS, 16, 16, 128), F32),
-            vm((STEPS, 16, 16, 128), F32),
             vm((STEPS, B, NY * words), BF),
+            vm((NY, words, blk // 4), BF),
+            vm((8, NY, 32, blk // 4), BF),
+            vm((7, NY, 32, blk // 4), BF),
+            vm((NY, 32, blk // 4), BF),
+            vm((3, 32, blk // 4), BF),
             vm((2, 8, 32, blk // 2), BF),
             vm((2, 7, 32, blk // 2), BF),
             vm((2, 8, 32, blk), BF),
@@ -420,9 +479,11 @@
             vm((2, NT, NX * NC, 16, rows // 2), BF),
             vm((NT, 4, 16, rows), F32),
             vm((2, NX * NC, 16, rows), F32),
-            dma((7,)),
+            dma((11,)),
             pltpu.SemaphoreType.REGULAR((4,)),
-            dma((2,)), dma((2,)),
+            dma((3,)), dma((3,)),
+            dma((1,)), dma((1,)),
+            dma((1,)), dma((1,)),
             dma((2,)), dma((2,)),
             dma((2,)), dma((2,)),
             dma((2,)), dma((2,)),

time: 93.8 us -> 91.1 us (0.971)
  Pallas kernels: 90.4 us -> 87.7 us
    pallas_call x1, Pallas kernels: 90.4 us -> 87.7 us  [per_device(): pl.pallas_call(kernel, out_shape=(jax.ShapeDtypeStruct((rows, cols), F32)...]
where the time goes in v4:
time: 91.1 us; the launch traced here: 91 us
  Pallas kernels  87.7 us (96%)
  local copies, waits for them, and re-layouts  2.64 us (3%)
    pallas_call x1, Pallas kernels, per_device(): pl.pallas_call(kernel, out_shape=(jax.ShapeDtypeStruct((rows, cols), F32)...  87.7 us
    unnamed x2, local copies, waits for them, and re-layouts  2.64 us

profile of v4, /device:TPU:1, one launch (start us, length us, event | category | flops | bytes accessed | tf_op | source)
XLA Modules:
  0.0 91.0 jit_solution(6970305264612626863)
XLA Ops:
  0.6 87.7 %window.1 = (f32[512,2048]{1,0:T(8,128)S(1)}, f32[32,512]{1,0:T(8,128)S(1)}) custom-call(bf16[512,2048]{1,0:T(8,128)(2,1)} %trans.1, bf16[256,2048]{1,0:T(8,128)(2,1)} %emis.1, bf16[3,256,512]{2,1,0:T(8,128)(2,1)} %forw.1, bf16[256,2048]{1,0:T(8,128)(2,1)} %beta.1, f32[3,256]{1,0:T(4,128)} %scales_in.1, s32[3,256]{1,0:T(4,128)} %tokens_in.1), custom_call_target="tpu_custom_call" | custom-call | tf_op jit(solution)/shard_map/window/pallas_call | solution.py:444
  88.3 2.0 %copy.10 = f32[512,2048]{1,0:T(8,128)} copy(f32[512,2048]{1,0:T(8,128)S(1)} %get-tuple-element.4) | data formatting | bytes 8388608
  90.4 0.6 copy.11

commit v5 on v4

--- a/solution.py
+++ b/solution.py
@@ -143,31 +143,36 @@
                 at = j * words + t * 128
                 hot[k, :, at : at + 128] = jnp.where(tok == lane, 1.0, 0.0).astype(BF)
 
+    def greet_ring(j):
+        greet(rdy.at[j], z_near)
+
+    def greeted_ring(j):
+        pl.semaphore_wait(rdy.at[j], 2)
+
+    greet_ring(0)
+    greet(rdy.at[3], x_near)
     loads[6].wait()
     hot_rows(2)
     for cp in corner:
         cp.wait()
     mine_hot = hot[2, :, pl.ds(pl.multiple_of(y * words, words), words)]
     for j in range(NY):
+        if j in (0, 2):
+            greeted_ring(j // 2)
+            greet_ring(j // 2 + 1)
         xb[:, j] = (
             jnp.dot(mine_hot, eb[j], preferred_element_type=F32).astype(BF).reshape(8, 32, qb_)
         )
-    for j in range(3):
-        greet(rdy.at[j], z_near)
-        pl.semaphore_wait(rdy.at[j], 2)
+    greeted_ring(2)
     for i in FAR:
         send(xb.at[zp(i)], rzb.at[i - 1], zb_s.at[0], zb_r.at[0], dev(x, y, zp(i), c))
     sent_all(rzb, zb_s.at[0])
 
+    for k in (1, 0):
+        hot_rows(k)
     for cp in loads[2:6]:
         cp.wait()
-    for k in (2, 1, 0):
-        sc[k] = as_column(scales[k : k + 1, :]).reshape(16, 16, 128)
-        if k < 2:
-            hot_rows(k)
-    for k in range(STEPS):
-        ft[:, k * B : (k + 1) * B] = fv[k].astype(F32).T.astype(BF)
-    greet(rdy.at[3], x_near)
+    sc[2] = as_column(scales[2:3, :]).reshape(16, 16, 128)
     pl.semaphore_wait(rdy.at[3], 2)
 
     def lookup(k, h, size):
@@ -263,6 +268,10 @@
     for t in range(NT):
         y_send(2, t)
     spread(0)
+    for k in (1, 0):
+        sc[k] = as_column(scales[k : k + 1, :]).reshape(16, 16, 128)
+    for k in range(STEPS):
+        ft[:, k * B : (k + 1) * B] = fv[k].astype(F32).T.astype(BF)
 
     def wait_rows(k, t):
         if k == 2 and t == 0:

time: 91.1 us -> 91.1 us (level)
  no operation moved by 1% of the time
where the time goes in v5:
time: 91.1 us; the launch traced here: 91 us
  Pallas kernels  87.7 us (96%)
  local copies, waits for them, and re-layouts  2.64 us (3%)
    pallas_call x1, Pallas kernels, per_device(): pl.pallas_call(kernel, out_shape=(jax.ShapeDtypeStruct((rows, cols), F32)...  87.7 us
    unnamed x2, local copies, waits for them, and re-layouts  2.64 us

profile of v5, /device:TPU:1, one launch (start us, length us, event | category | flops | bytes accessed | tf_op | source)
XLA Modules:
  0.0 91.0 jit_solution(13145343005610141633)
XLA Ops:
  0.6 87.7 %window.1 = (f32[512,2048]{1,0:T(8,128)S(1)}, f32[32,512]{1,0:T(8,128)S(1)}) custom-call(bf16[512,2048]{1,0:T(8,128)(2,1)} %trans.1, bf16[256,2048]{1,0:T(8,128)(2,1)} %emis.1, bf16[3,256,512]{2,1,0:T(8,128)(2,1)} %forw.1, bf16[256,2048]{1,0:T(8,128)(2,1)} %beta.1, f32[3,256]{1,0:T(4,128)} %scales_in.1, s32[3,256]{1,0:T(4,128)} %tokens_in.1), custom_call_target="tpu_custom_call" | custom-call | tf_op jit(solution)/shard_map/window/pallas_call | solution.py:453
  88.4 2.0 %copy.10 = f32[512,2048]{1,0:T(8,128)} copy(f32[512,2048]{1,0:T(8,128)S(1)} %get-tuple-element.4) | data formatting | bytes 8388608
  90.4 0.6 copy.11

commit v6 on v5

--- a/solution.py
+++ b/solution.py
@@ -10,6 +10,7 @@
 B = 256
 STEPS = 3
 NT = 4
+SPLIT = (0, 3)
 BF = jnp.bfloat16
 F32 = jnp.float32
 FAR = (4, 3, 5, 2, 6, 1, 7)
@@ -28,7 +29,7 @@
     w, own, pb, pr, qb, orx, fp, fx,
     l_sem, rdy,
     e_s, e_r, zb_s, zb_r, yb_s, yb_r, z2_s, z2_r, zw_s, zw_r, z10_s, z10_r, pm_s, pm_r,
-    ya_s, ya_r, y_s, y_r, pp_s, pp_r, o_s, o_r, zz_s, zz_r, fx_s, fx_r,
+    ya_s, ya_r, y_s, y_r, pp_s, pp_r, o_s, o_r, zz_s, zz_r, fx_s, fx_r, ls_s, ls_r,
 ):
     s = lax.axis_index("src")
     d = lax.axis_index("dst")
@@ -45,6 +46,7 @@
     oc = z // 4
     q = z % 4
     qo = pl.multiple_of(q * blk, blk)
+    qo_late = pl.multiple_of(q * blk + hb, hb)
     is_owner = c == oc
 
     def zp(i):
@@ -257,7 +259,7 @@
         return w.at[k, yt, t]
 
     def y_three(k, t):
-        return w.at[2, 0:3, t, :, 0 : 4 * hb] if k == 2 else w.at[k, 0:3, t]
+        return w.at[k, 0:3, t, :, 0 : 4 * hb] if k == 2 or (k, t) == SPLIT else w.at[k, 0:3, t]
 
     def y_send(k, t):
         part = y_part(k, t, y)
@@ -277,6 +279,9 @@
         if k == 2 and t == 0:
             arrive(three_a, ya_r.at[0])
         arrive(y_three(k, t), y_r.at[k, t])
+        if (k, t) == SPLIT:
+            arrive(w.at[k, 0:3, t, :, 0 : 4 * hb], ls_r.at[1], is_owner)
+            arrive(w.at[k, :, t, :, 0 : 4 * hb], ls_r.at[1], jnp.logical_not(is_owner))
 
     def product(k, t, j):
         return jnp.dot(
@@ -351,12 +356,38 @@
                 em[k, t // 2, lo : lo + 16].astype(F32) * msg, k, 4 * y + t
             ).astype(BF)
 
+        if (k, t) == SPLIT:
+            tile = w.at[k, y, t, :, pl.ds(qo, hb)]
+            other = w.at[k, y, t, :, pl.ds(qo_late, hb)]
+            for i in (2, 1, 3):
+                send(other, other, ls_s.at[0], ls_r.at[0], dev(x, yp(i), z, c), is_owner)
+            sent_all(w.at[k, 0, t, :, 0 : 3 * hb], ls_s.at[0], is_owner)
+            for i in FAR:
+                send(tile, tile, zz_s.at[k, t], zz_r.at[k, t], dev(x, y, zp(i), c), is_owner)
+            sent_all(rz2.at[0, :, :, 0:qb_], zz_s.at[k, t], is_owner)
+            return
         tile = w.at[k, y, t, :, pl.ds(qo, blk)]
         for i in FAR:
             send(tile, tile, zz_s.at[k, t], zz_r.at[k, t], dev(x, y, zp(i), c), is_owner)
         sent_all(rz2.at[0], zz_s.at[k, t], is_owner)
 
+    def across(k, t):
+        arrive(w.at[k, 0, t, :, 0 : 3 * hb], ls_r.at[0], is_owner)
+        part = w.at[k, :, t, :, pl.ds(qo_late, hb)]
+        for i in FAR:
+            send(part, part, ls_s.at[1], ls_r.at[1], dev(x, y, zp(i), c), is_owner)
+        sent_all(rz10.at[0], ls_s.at[1], is_owner)
+
     def column(k, t):
+        if (k, t) == SPLIT:
+            arrive(w.at[k, y, t, :, 0 : 3 * hb], zz_r.at[k, t], is_owner)
+            arrive(w.at[k, y, t, :, 0 : 4 * hb], zz_r.at[k, t], jnp.logical_not(is_owner))
+            for j in range(4):
+                part = w.at[k, y, t, :, j * blk : j * blk + hb]
+                for i in (2, 1, 3):
+                    send(part, part, y_s.at[k, t], y_r.at[k, t], dev(x, yp(i), z, c))
+            sent_all(y_three(k, t), y_s.at[k, t])
+            return
         arrive(w.at[k, y, t, :, 0 : 3 * blk], zz_r.at[k, t], is_owner)
         arrive(w.at[k, y, t], zz_r.at[k, t], jnp.logical_not(is_owner))
         y_send(k, t)
@@ -413,6 +444,7 @@
     column(0, 1)
     column(0, 2)
     last(0)
+    across(0, 3)
     column(0, 3)
     last(1)
     last(2)
@@ -503,6 +535,7 @@
             dma((2, NT)), dma((2, NT)),
             dma((2, NT)), dma((2, NT)),
             dma((NT,)), dma((2,)),
+            dma((2,)), dma((2,)),
         ],
         compiler_params=pltpu.CompilerParams(
             collective_id=0, has_side_effects=True, vmem_limit_bytes=30 * 1024 * 1024

time: 91.1 us -> 90.6 us (level)
  no operation moved by 1% of the time
where the time goes in v6:
time: 90.6 us; the launch traced here: 90.5 us
  Pallas kernels  87.2 us (96%)
  local copies, waits for them, and re-layouts  2.64 us (3%)
    pallas_call x1, Pallas kernels, per_device(): pl.pallas_call(kernel, out_shape=(jax.ShapeDtypeStruct((rows, cols), F32)...  87.2 us
    unnamed x2, local copies, waits for them, and re-layouts  2.64 us

profile of v6, /device:TPU:1, one launch (start us, length us, event | category | flops | bytes accessed | tf_op | source)
XLA Modules:
  0.0 90.5 jit_solution(9623668378804673758)
XLA Ops:
  0.6 87.2 %window.1 = (f32[512,2048]{1,0:T(8,128)S(1)}, f32[32,512]{1,0:T(8,128)S(1)}) custom-call(bf16[512,2048]{1,0:T(8,128)(2,1)} %trans.1, bf16[256,2048]{1,0:T(8,128)(2,1)} %emis.1, bf16[3,256,512]{2,1,0:T(8,128)(2,1)} %forw.1, bf16[256,2048]{1,0:T(8,128)(2,1)} %beta.1, f32[3,256]{1,0:T(4,128)} %scales_in.1, s32[3,256]{1,0:T(4,128)} %tokens_in.1), custom_call_target="tpu_custom_call" | custom-call | tf_op jit(solution)/shard_map/window/pallas_call | solution.py:485
  87.8 2.0 %copy.10 = f32[512,2048]{1,0:T(8,128)} copy(f32[512,2048]{1,0:T(8,128)S(1)} %get-tuple-element.4) | data formatting | bytes 8388608
  89.9 0.6 copy.11
